TPU v7x, 256 devices: a whole 4x4x8 slice. The times are simulated.
256 devices in a mesh: ctx: 32 (over y, z), head: 8 (over x, core).
Axes of the slice: x: 4, y: 4, z: 8, core: 2. Of those that a mesh axis runs over, the one named last changes fastest.
Arguments:
- lin_q: bfloat16 [4096, 32, 128], P('ctx', 'head'), may hold values from -4 to 4
- lin_k: bfloat16 [4096, 32, 128], P('ctx', 'head'), may hold values from -4 to 4
- lin_v: bfloat16 [4096, 32, 128], P('ctx', 'head'), may hold values from -16 to 16
- lin_decay: float32 [32, 4096], P('head', 'ctx'), may hold values from -1.5 to 0
- norm_gain: float32 [32, 128], P('head'), may hold values from 0.1 to 1.9
- soft_q: bfloat16 [4096, 32, 128], P('ctx', 'head'), may hold values from -5 to 5
- soft_k: bfloat16 [4096, 32, 128], P('ctx', 'head'), may hold values from -5 to 5
- soft_v: bfloat16 [4096, 32, 128], P('ctx', 'head'), may hold values from -5 to 5
- out_grad: bfloat16 [4096, 32, 128], P('ctx', 'head'), may hold values from -5 to 5
- block_lists: int32 [32, 16], P('ctx'), may hold values from 0 to 30, as said below
- block_counts: int32 [32], P('ctx'), may hold values from 0 to 16, as said below
Outputs:
- lin_dq: bfloat16 [4096, 32, 128], P('ctx', 'head')
- lin_dk: bfloat16 [4096, 32, 128], P('ctx', 'head')
- lin_dv: bfloat16 [4096, 32, 128], P('ctx', 'head')
- soft_dq: bfloat16 [4096, 32, 128], P('ctx', 'head')
- soft_dk: bfloat16 [4096, 32, 128], P('ctx', 'head')
- soft_dv: bfloat16 [4096, 32, 128], P('ctx', 'head')
Inputs may be any that keep to these rules, and one draw needn't show every extreme that they name: `block_lists`: entries past block_counts[b] are 0. The first block_counts[b] entries of query block b are distinct blocks that lie before the span of 128 tokens holding b. All query blocks of one span name together at most one block of each other span. In every span after the first, some query block names every block that its span names; from the second span on these include block 0, and from the third on also the last block before the span. `block_counts`: in span i of 128 tokens some query block has the count min(i, 16); every count is at most that; counts are 0 only in the first span.
All inputs are finite; a program needn't handle non-finite values.
Results may differ from a plain program's by a relative error of at most 0.011.
Values may be sent and summed in bfloat16 or wider, within the bound.
A program may use at most 128 MiB of HBM per device.

v0:
```python
import jax
import jax.numpy as jnp
from jax import lax
from jax.sharding import PartitionSpec as P

BLK = 128
NSEL = 16
epsilon = 1e-05
exact_precision = lax.Precision.HIGHEST


def carried_in(part, axis, combine, identity, reverse):
    count = lax.axis_size(axis)
    place = lax.axis_index(axis)
    ahead = count - 1 - place if reverse else place
    gathered = jax.tree.map(lambda a: lax.all_gather(a, axis), part)
    state = jax.tree.map(lambda a, e: jnp.zeros_like(a) + jnp.asarray(e, a.dtype), part, identity)

    def one(lap, state):
        source = count - 1 - lap if reverse else lap
        return combine(
            state, jax.tree.map(lambda a: lax.dynamic_index_in_dim(a, source, 0, False), gathered)
        )

    return lax.fori_loop(0, ahead, one, state)


def decay_tables(decays):
    running = jnp.cumsum(decays, axis=1)
    finish = running[:, -1]
    length = decays.shape[1]
    below_diag = (jnp.arange(length)[:, None] >= jnp.arange(length)[None, :])[None]
    spread = running[:, :, None] - running[:, None, :]
    within = jnp.where(below_diag, jnp.exp(jnp.where(below_diag, spread, 0.0)), 0.0)
    return (jnp.exp(finish), jnp.exp(finish[:, None] - running), jnp.exp(running), within)


def chain_join(earlier, later):
    return (earlier[0] * later[0], later[0][:, None, None] * earlier[1] + later[1])


def sparse_grads(queries, grads_out, key_rows, value_rows, allowed):
    score_scale = queries.shape[-1] ** (-0.5)
    scores = (
        jnp.einsum("bqhd,bkhd->bhqk", queries, key_rows, preferred_element_type=jnp.float32)
        * score_scale
    )
    key_mask = allowed[:, None]
    scores = jnp.where(key_mask, scores, -1e30)
    row_max = jnp.max(scores, axis=-1, keepdims=True)
    weights = jnp.where(key_mask, jnp.exp(scores - row_max), 0.0)
    softmax_probs = weights / jnp.sum(weights, axis=-1, keepdims=True)
    rounded = softmax_probs.astype(jnp.bfloat16)
    outputs = jnp.einsum("bhqk,bkhd->bqhd", rounded, value_rows, preferred_element_type=jnp.float32)
    row_delta = jnp.sum(grads_out.astype(jnp.float32) * outputs, axis=-1)
    grad_probs = jnp.einsum(
        "bqhd,bkhd->bhqk", grads_out, value_rows, preferred_element_type=jnp.float32
    )
    grad_scores = (
        softmax_probs * (grad_probs - jnp.transpose(row_delta, (0, 2, 1))[..., None])
    ).astype(jnp.bfloat16)
    query_gradient = (
        jnp.einsum("bhqk,bkhd->bqhd", grad_scores, key_rows, preferred_element_type=jnp.float32)
        * score_scale
    )
    key_gradient = (
        jnp.einsum("bhqk,bqhd->bkhd", grad_scores, queries, preferred_element_type=jnp.float32)
        * score_scale
    )
    value_gradient = jnp.einsum(
        "bhqk,bqhd->bkhd", rounded, grads_out, preferred_element_type=jnp.float32
    )
    return (query_gradient, key_gradient, value_gradient)


def local(
    lin_q,
    lin_k,
    lin_v,
    lin_decay,
    norm_gain,
    soft_q,
    soft_k,
    soft_v,
    out_grad,
    block_lists,
    block_counts,
):
    tok_rows, heads_here, head_width = lin_q.shape
    blocks_here = tok_rows // BLK
    span_count = lax.axis_size("ctx")
    own_span = lax.axis_index("ctx")
    total_width = heads_here * lax.axis_size("head") * head_width
    complete_query = lin_q.astype(jnp.float32)
    complete_key = lin_k.astype(jnp.float32)
    complete_value = lin_v.astype(jnp.float32)
    carry_decay, trailing_decay, leading_decay, within = decay_tables(lin_decay)
    state_here = jnp.einsum(
        "boz,bor->ozr",
        complete_key * trailing_decay.T[:, :, None],
        complete_value,
        precision=exact_precision,
    )
    identity = (jnp.ones_like(carry_decay), jnp.zeros_like(state_here))
    incoming_state = carried_in((carry_decay, state_here), "ctx", chain_join, identity, False)[1]
    pair_weights = (
        jnp.einsum("thk,shk->hts", lin_q, lin_k, preferred_element_type=jnp.float32) * within
    )
    layer_out = jnp.einsum("hts,shv->thv", pair_weights, complete_value, precision=exact_precision)
    layer_out = layer_out + leading_decay.T[:, :, None] * jnp.einsum(
        "wfg,fgl->wfl", complete_query, incoming_state, precision=exact_precision
    )
    squares = lax.psum(jnp.sum(layer_out * layer_out, axis=(1, 2)), "head")
    root_mean = jnp.sqrt(squares / total_width + epsilon)
    norm_scale = norm_gain[None]
    all_lists, all_counts = (
        lax.all_gather(block_lists, "ctx", axis=0, tiled=True),
        lax.all_gather(block_counts, "ctx", axis=0, tiled=True),
    )
    entries = blocks_here * NSEL
    every_live = (
        jnp.arange(NSEL)[None, None, :] < all_counts.reshape(span_count, blocks_here)[:, :, None]
    ).reshape(span_count, entries)
    owner_hits = every_live & (all_lists // blocks_here == own_span)
    wanted_here = jnp.max(jnp.where(owner_hits, all_lists % blocks_here, -1), axis=1)
    my_live = jnp.arange(NSEL)[None, :] < block_counts[:, None]
    flat_owner = (block_lists // blocks_here).reshape(entries)
    flat_live = my_live.reshape(entries)
    key_blocks = soft_k.reshape(blocks_here, BLK, heads_here, head_width)
    value_blocks = soft_v.reshape(blocks_here, BLK, heads_here, head_width)
    owners = jnp.arange(span_count)
    matches = flat_live[None, :] & (flat_owner[None, :] == owners[:, None])
    wanted_ids = jnp.max(jnp.where(matches, block_lists.reshape(entries)[None, :], -1), axis=1)
    empty_slot = jnp.zeros((span_count, BLK, heads_here, head_width), jnp.bfloat16)
    shard_piece = (
        lax.all_gather(soft_k, "ctx", axis=0, tiled=True),
        lax.all_gather(soft_v, "ctx", axis=0, tiled=True),
    )
    row_count = shard_piece[0].shape[0]
    token_index = wanted_ids[:, None] * BLK + jnp.arange(BLK)[None, :]
    usable = ((wanted_ids[:, None] >= 0) & (token_index >= 0) & (token_index < row_count))[
        :, :, None, None
    ]
    safe_index = jnp.clip(token_index, 0, row_count - 1)
    new_keys = jnp.where(usable, shard_piece[0][safe_index], empty_slot)
    new_values = jnp.where(usable, shard_piece[1][safe_index], empty_slot)
    listed_keys = jnp.take(new_keys, flat_owner, axis=0).reshape(
        blocks_here, NSEL * BLK, heads_here, head_width
    )
    listed_values = jnp.take(new_values, flat_owner, axis=0).reshape(
        blocks_here, NSEL * BLK, heads_here, head_width
    )
    key_rows = jnp.concatenate([key_blocks, listed_keys], axis=1)
    value_rows = jnp.concatenate([value_blocks, listed_values], axis=1)
    causal = jnp.arange(BLK)[:, None] >= jnp.arange(BLK)[None, :]
    remote_mask = jnp.broadcast_to(
        jnp.repeat(my_live, BLK, axis=1)[:, None, :], (blocks_here, BLK, NSEL * BLK)
    )
    allowed = jnp.concatenate(
        [jnp.broadcast_to(causal, (blocks_here, BLK, BLK)), remote_mask], axis=2
    )
    query_blocks = soft_q.reshape(blocks_here, BLK, heads_here, head_width)
    grad_blocks = out_grad.reshape(blocks_here, BLK, heads_here, head_width)
    query_gradient, key_gradient, value_gradient = sparse_grads(
        query_blocks, grad_blocks, key_rows, value_rows, allowed
    )
    soft_dq = query_gradient.reshape(tok_rows, heads_here, head_width).astype(jnp.bfloat16)
    routing = (
        flat_live[None, :] & (flat_owner[None, :] == jnp.arange(span_count)[:, None])
    ).astype(jnp.float32)
    remote_key = key_gradient[:, BLK:].reshape(entries, BLK, heads_here, head_width)
    remote_value = value_gradient[:, BLK:].reshape(entries, BLK, heads_here, head_width)
    part_key = jnp.einsum("oe,exhd->oxhd", routing, remote_key, precision=exact_precision).astype(
        jnp.bfloat16
    )
    part_value = jnp.einsum(
        "oe,exhd->oxhd", routing, remote_value, precision=exact_precision
    ).astype(jnp.bfloat16)
    back_key, back_value = (
        lax.all_to_all(part_key, "ctx", split_axis=0, concat_axis=0, tiled=True),
        lax.all_to_all(part_value, "ctx", split_axis=0, concat_axis=0, tiled=True),
    )
    placing = (wanted_here[:, None] == jnp.arange(blocks_here)[None, :]).astype(jnp.float32)
    added_key = jnp.einsum(
        "rb,rxhd->bxhd", placing, back_key.astype(jnp.float32), precision=exact_precision
    ).reshape(tok_rows, heads_here, head_width)
    added_value = jnp.einsum(
        "rb,rxhd->bxhd", placing, back_value.astype(jnp.float32), precision=exact_precision
    ).reshape(tok_rows, heads_here, head_width)
    soft_dk = (key_gradient[:, :BLK].reshape(tok_rows, heads_here, head_width) + added_key).astype(
        jnp.bfloat16
    )
    value_total = value_gradient[:, :BLK].reshape(tok_rows, heads_here, head_width) + added_value
    soft_dv = value_total.astype(jnp.bfloat16)
    cotangent = out_grad.astype(jnp.float32) + value_total
    inner_total = lax.psum(jnp.sum(norm_scale * cotangent * layer_out, axis=(1, 2)), "head")
    linear_cotangent = (
        norm_scale * cotangent / root_mean[:, None, None]
        - layer_out * (inner_total / (total_width * root_mean**3))[:, None, None]
    )
    reverse_state = carried_in(
        (
            carry_decay,
            jnp.einsum(
                "boz,bor->ozr",
                complete_query * leading_decay.T[:, :, None],
                linear_cotangent,
                precision=exact_precision,
            ),
        ),
        "ctx",
        chain_join,
        identity,
        True,
    )[1]
    grad_pair = (
        jnp.einsum("thv,shv->hts", linear_cotangent, complete_value, precision=exact_precision)
        * within
    )
    lin_dq = jnp.einsum("hts,shk->thk", grad_pair, complete_key, precision=exact_precision)
    lin_dq = lin_dq + leading_decay.T[:, :, None] * jnp.einsum(
        "fqs,qrs->fqr", linear_cotangent, incoming_state, precision=exact_precision
    )
    lin_dk = jnp.einsum("hts,thk->shk", grad_pair, complete_query, precision=exact_precision)
    lin_dk = lin_dk + trailing_decay.T[:, :, None] * jnp.einsum(
        "fut,ujt->fuj", complete_value, reverse_state, precision=exact_precision
    )
    lin_dv = jnp.einsum("hts,thv->shv", pair_weights, linear_cotangent, precision=exact_precision)
    lin_dv = lin_dv + trailing_decay.T[:, :, None] * jnp.einsum(
        "zpu,pux->zpx", complete_key, reverse_state, precision=exact_precision
    )
    return (
        lin_dq.astype(jnp.bfloat16),
        lin_dk.astype(jnp.bfloat16),
        lin_dv.astype(jnp.bfloat16),
        soft_dq,
        soft_dk,
        soft_dv,
    )


def solution(mesh):
    in_specs = (
        P("ctx", "head", None),
        P("ctx", "head", None),
        P("ctx", "head", None),
        P("head", "ctx"),
        P("head", None),
        P("ctx", "head", None),
        P("ctx", "head", None),
        P("ctx", "head", None),
        P("ctx", "head", None),
        P("ctx", None),
        P("ctx"),
    )
    out_specs = (
        P("ctx", "head", None),
        P("ctx", "head", None),
        P("ctx", "head", None),
        P("ctx", "head", None),
        P("ctx", "head", None),
        P("ctx", "head", None),
    )
    return jax.shard_map(local, mesh=mesh, in_specs=in_specs, out_specs=out_specs, check_vma=False)
```

profile of v0, /device:TPU:32, one launch (start us, length us, event | category | flops | bytes accessed | tf_op | source)
XLA Modules:
  0.0 770.6 jit_solution(8444766852220716513)
XLA Ops:
  11.1 2.1 fusion.51
  17.2 1.3 add_bitcast_fusion
  18.5 76.2 %all-gather.11.cloned.1.call-done = bf16[4096,4,128]{2,1,0:T(4,128)(2,1)} async-done(((bf16[128,4,128]{2,1,0:T(4,128)(2,1)}), bf16[4096,4,128]{2,1,0:T(4,128)(2,1)}) %all-gather.11.cloned.1.call-update) | async-done | bytes 4194320 | tf_op jit(solution)/shard_map/all_gather | solution.py:137
  94.7 30.5 %gather_fusion.1 = bf16[4096,4,128]{2,1,0:T(4,128)(2,1)} fusion(bf16[4096,4,128]{2,1,0:T(4,128)(2,1)} %all-gather.11.cloned.1.call-done, s32[4096]{0:T(1024)S(1)} %fusion.73), kind=kCustom, calls=%fused_computation.3 | custom fusion | bytes 8404992 | tf_op jit(solution)/shard_map/gather | solution.py:146
  125.2 50.7 %all-gather.9.cloned.1.call-done = bf16[4096,4,128]{2,1,0:T(4,128)(2,1)} async-done(((bf16[128,4,128]{2,1,0:T(4,128)(2,1)}), bf16[4096,4,128]{2,1,0:T(4,128)(2,1)}) %all-gather.9.cloned.1.call-update) | async-done | bytes 4194320 | tf_op jit(solution)/shard_map/all_gather | solution.py:136
  175.9 30.5 %gather_fusion = bf16[4096,4,128]{2,1,0:T(4,128)(2,1)} fusion(bf16[4096,4,128]{2,1,0:T(4,128)(2,1)} %all-gather.9.cloned.1.call-done, s32[4096]{0:T(1024)S(1)} %fusion.73), kind=kCustom, calls=%fused_computation.2 | custom fusion | bytes 8404992 | tf_op jit(solution)/shard_map/gather | solution.py:145
  206.4 6.7 copy_select_fusion
  213.0 3.2 gather_fusion.3
  216.2 4.4 gather_fusion.2
  220.6 3.4 broadcast_select_fusion
  224.2 3.9 fusion.102
  228.1 2.7 fusion.24
  231.8 1.7 copy-done.1
  233.5 7.4 fusion.18
  241.0 4.2 copy.213
  245.2 6.6 all-to-all-start
  253.3 170.3 %all-reduce.1 = f32[128]{0:T(128)S(1)} all-reduce(f32[128]{0:T(128)S(1)} %dynamic-update-slice.1), channel_id=2, replica_groups=mesh['ctx'=32,'head'=8] {'ctx'}, use_global_device_ids=true, to_apply=%add.1 | all-reduce | flops 128 | bytes 1024
  423.8 37.6 %all-gather.3 = s32[32,1,16]{2,1,0:T(1,128)S(1)} all-gather(s32[1,1,16]{2,1,0:T(1,128)S(1)} %bitcast.233), channel_id=1, replica_groups=mesh['ctx'=32,'head'=8] {'ctx'}, dimensions={0}, use_global_device_ids=true | all-gather | bytes 2112 | tf_op jit(solution)/shard_map/all_gather | solution.py:117
  462.2 18.1 %all-reduce = s32[32]{0:T(128)S(1)} all-reduce(s32[32]{0:T(128)S(1)} %dynamic-update-slice), channel_id=1, replica_groups=mesh['ctx'=32,'head'=8] {'ctx'}, use_global_device_ids=true, to_apply=%add | all-reduce | flops 32 | bytes 256
  482.1 1.1 while.26
  482.1 1.1 bitcast_add_fusion.4
  483.8 4.6 fusion.12
  488.4 2.0 multiply_reduce_fusion.1
  490.5 12.6 %all-reduce.2 = (f32[128]{0:T(128)S(1)}, f32[128]{0:T(128)S(1)}) all-reduce(f32[128]{0:T(128)S(1)} %get-tuple-element.168, f32[128]{0:T(128)S(1)} %get-tuple-element.167), channel_id=1, replica_groups=mesh['ctx'=32,'head'=8] {'head'}, use_global_device_ids=true, to_apply=%region_10.12 | all-reduce | flops 256 | bytes 2048 | tf_op jit(solution)/shard_map/psum | solution.py:196
  503.1 1.2 multiply_subtract_fusion
  504.4 2.1 fusion.48
  507.4 1.8 copy.241
  509.2 1.9 fusion.43
  511.1 3.1 fusion.9
  515.2 1.8 copy-done.2
  517.0 7.2 fusion.21
  524.3 4.1 copy.250
  528.4 38.5 %all-to-all-start.1 = ((bf16[32,128,4,128]{3,2,1,0:T(4,128)(2,1)}), bf16[32,128,4,128]{3,2,1,0:T(4,128)(2,1)}, u32[]{:S(2)}, u32[]{:S(2)}) async-start(bf16[32,128,4,128]{3,2,1,0:T(4,128)(2,1)} %copy.250), calls=%async_computation.1 | async-start | bytes 8388608 | tf_op jit(solution)/shard_map/all_to_all | solution.py:180
  566.9 2.5 fusion.42
  570.2 128.2 %all-to-all-done.1 = bf16[32,128,4,128]{3,2,1,0:T(4,128)(2,1)} async-done(((bf16[32,128,4,128]{3,2,1,0:T(4,128)(2,1)}), bf16[32,128,4,128]{3,2,1,0:T(4,128)(2,1)}, u32[]{:S(2)}, u32[]{:S(2)}) %all-to-all-start.1) | async-done | bytes 4194336 | tf_op jit(solution)/shard_map/all_to_all | solution.py:180
  698.3 4.6 fusion.10
  708.6 53.2 %while.27 = (s32[]{:T(128)}, f32[4,128,128]{2,1,0:T(8,128)S(1)}, s32[]{:T(128)}, f32[32,4]{1,0:T(8,128)}, f32[32,4,128,128]{3,2,1,0:T(8,128)}, /*index=5*/s32[]{:T(128)}, s32[]{:T(128)}, s32[]{:T(128)}, s32[]{:T(128)}) while((s32[]{:T(128)}, f32[4,128,128]{2,1,0:T(8,128)S(1)}, s32[]{:T(128)}, f32[32,4]{1,0:T(8,128)}, ...), condition=%wide.region_12.14_spmd, body=%wide.region_11.13_spmd.sunk | while | flops 131078 | bytes 786635 | solution.py:25
  709.3 1.1 bitcast_add_fusion.5
  711.1 1.1 bitcast_add_fusion.5
  712.9 1.1 bitcast_add_fusion.5
  714.6 1.1 bitcast_add_fusion.5
  716.4 1.1 bitcast_add_fusion.5
  718.2 1.1 bitcast_add_fusion.5
  720.0 1.1 bitcast_add_fusion.5
  721.7 1.1 bitcast_add_fusion.5
  723.5 1.1 bitcast_add_fusion.5
  727.1 1.1 bitcast_add_fusion.5
  728.8 1.1 bitcast_add_fusion.5
  (165 shorter events, 63.9 us)
Async XLA Ops:
  7.2 217.0 %copy-start = (bf16[128,4,128]{2,1,0:T(4,128)(2,1)S(1)}, bf16[128,4,128]{2,1,0:T(4,128)(2,1)}, u32[]{:S(2)}) copy-start(bf16[128,4,128]{2,1,0:T(4,128)(2,1)} %param.22) | copy-start | bytes 393220
  7.2 87.5 %all-gather.11.cloned.1.call-start = ((), (), s32[]{:S(2)}) async-start(), calls=%async_computation.3 | async-start | bytes 4325376 | tf_op jit(solution)/shard_map/all_gather | solution.py:137
  7.9 168.0 %all-gather.9.cloned.1.call-start = ((), (), s32[]{:S(2)}) async-start(), calls=%async_computation.2 | async-start | bytes 4325376 | tf_op jit(solution)/shard_map/all_gather | solution.py:136
  8.7 473.4 %all-gather.13.cloned.1.call-start = ((), (), s32[]{:S(2)}) async-start(), calls=%async_computation.4 | async-start | bytes 8650752 | tf_op jit(solution)/shard_map/all_gather | solution.py:16
  9.7 471.1 %copy-start.15 = (f32[4,128]{1,0:T(4,128)}, f32[4,128]{1,0:T(4,128)S(1)}, u32[]{:S(2)}) copy-start(f32[4,128]{1,0:T(4,128)S(1)} %reduce_window_sum.11) | copy-start | bytes 6148
  10.5 0.6 copy-start.17
  14.2 210.0 %copy-start.13 = (bf16[128,4,128]{2,0,1:T(8,128)(2,1)}, bf16[128,4,128]{2,0,1:T(8,128)(2,1)S(1)}, u32[]{:S(2)}) copy-start(bf16[128,4,128]{2,0,1:T(8,128)(2,1)S(1)} %copy.353) | copy-start | bytes 393220
  14.8 218.7 %copy-start.23 = (pred[16]{0:T(512)(128)(4,1)}, pred[16]{0:T(512)(128)(4,1)S(1)}, u32[]{:S(2)}) copy-start(pred[16]{0:T(512)(128)(4,1)S(1)} %iota_compare_fusion.4) | copy-start | bytes 52
  224.2 3.9 copy-start.3
  228.1 3.4 copy-start.25
  228.1 2.7 copy-start.7
  231.5 2.0 copy-start.1
  231.5 2.0 copy-start.21
  245.1 6.7 copy-start.27
  245.1 235.7 %copy-start.5 = (bf16[128,4,128]{2,1,0:T(4,128)(2,1)S(1)}, bf16[128,4,128]{2,1,0:T(4,128)(2,1)}, u32[]{:S(2)}) copy-start(bf16[128,4,128]{2,1,0:T(4,128)(2,1)} %param.17) | copy-start | bytes 393220
  245.2 235.7 %copy-start.6 = (bf16[128,4,128]{2,1,0:T(4,128)(2,1)S(1)}, bf16[128,4,128]{2,1,0:T(4,128)(2,1)}, u32[]{:S(2)}) copy-start(bf16[128,4,128]{2,1,0:T(4,128)(2,1)} %param.18) | copy-start | bytes 393220
  245.2 235.9 %copy-start.4 = (bf16[128,4,128]{2,1,0:T(4,128)(2,1)S(1)}, bf16[128,4,128]{2,1,0:T(4,128)(2,1)}, u32[]{:S(2)}) copy-start(bf16[128,4,128]{2,1,0:T(4,128)(2,1)} %param.19) | copy-start | bytes 393220
  245.2 238.6 %all-to-all-start = ((bf16[32,128,4,128]{3,2,1,0:T(4,128)(2,1)}), bf16[32,128,4,128]{3,2,1,0:T(4,128)(2,1)}, u32[]{:S(2)}, u32[]{:S(2)}) async-start(bf16[32,128,4,128]{3,2,1,0:T(4,128)(2,1)} %copy.213), calls=%async_computation | async-start | bytes 8388608 | tf_op jit(solution)/shard_map/all_to_all | solution.py:181
  251.8 456.8 %all-gather.15.cloned.1.call-start = ((), (), s32[]{:S(2)}) async-start(), calls=%async_computation.5 | async-start | bytes 8650752 | tf_op jit(solution)/shard_map/all_gather | solution.py:16
  481.1 2.1 copy-start.9
  483.2 0.6 copy-start.20
  483.8 4.7 copy-start.11
  509.2 1.9 copy-start.8
  509.2 1.9 copy-start.26
  514.9 2.1 copy-start.2
  514.9 2.1 copy-start.22
  514.9 2.1 copy-start.24
  528.4 38.5 %copy-start.14 = (bf16[128,4,128]{2,0,1:T(8,128)(2,1)S(1)}, bf16[128,4,128]{2,0,1:T(8,128)(2,1)}, u32[]{:S(2)}) copy-start(bf16[128,4,128]{2,0,1:T(8,128)(2,1)} %copy-done.13) | copy-start | bytes 393220
  528.4 170.0 %all-to-all-start.1 = ((bf16[32,128,4,128]{3,2,1,0:T(4,128)(2,1)}), bf16[32,128,4,128]{3,2,1,0:T(4,128)(2,1)}, u32[]{:S(2)}, u32[]{:S(2)}) async-start(bf16[32,128,4,128]{3,2,1,0:T(4,128)(2,1)} %copy.250), calls=%async_computation.1 | async-start | bytes 8388608 | tf_op jit(solution)/shard_map/all_to_all | solution.py:180
  569.4 135.3 %copy-start.12 = (bf16[128,4,128]{2,0,1:T(8,128)(2,1)S(1)}, bf16[128,4,128]{2,0,1:T(8,128)(2,1)}, u32[]{:S(2)}) copy-start(bf16[128,4,128]{2,0,1:T(8,128)(2,1)} %get-tuple-element.193) | copy-start | bytes 393220
  569.4 136.1 %copy-start.16 = (f32[4,128]{1,0:T(4,128)S(1)}, f32[4,128]{1,0:T(4,128)}, u32[]{:S(2)}) copy-start(f32[4,128]{1,0:T(4,128)} %copy-done.15) | copy-start | bytes 6148
  569.4 136.7 %copy-start.19 = (f32[128,4]{0,1:T(4,128)S(1)}, f32[128,4]{0,1:T(4,128)}, u32[]{:S(2)}) copy-start(f32[128,4]{0,1:T(4,128)} %get-tuple-element.196) | copy-start | bytes 6148
  570.2 137.8 %copy-start.10 = (f32[4,128,128]{2,1,0:T(8,128)S(1)}, f32[4,128,128]{2,1,0:T(8,128)}, u32[]{:S(2)}) copy-start(f32[4,128,128]{2,1,0:T(8,128)} %copy-done.9) | copy-start | bytes 786436
  705.5 56.4 %copy-start.18 = (f32[128,4]{0,1:T(4,128)S(1)}, f32[128,4]{0,1:T(4,128)}, u32[]{:S(2)}) copy-start(f32[128,4]{0,1:T(4,128)} %copy-done.17) | copy-start | bytes 6148
Sparse Core Ops, SparseCore 0:
  10.6 84.0 all-gather.10
  97.3 78.5 all-gather.8
  178.5 149.4 all-gather.12
  506.6 193.3 all-gather.14
where the time goes:
time: 773 us; the launch traced here: 771 us
  waiting for transfers between devices  256 us (33%)
  blocking collectives  239 us (31%)
  local copies, waits for them, and re-layouts  114 us (15%)
  other arithmetic  53.3 us (7%)
  matrix products  47 us (6%)
  starting transfers between devices  45.2 us (6%)
  between operations  15.6 us (2%)
    unnamed x2, blocking collectives  188 us
    all_to_all x1, waiting for transfers between devices, local(): lax.all_to_all(part_key, 'ctx', split_axis=0, concat_axis=0, tiled=True)  128 us
    all_gather x1, waiting for transfers between devices, local(): lax.all_gather(soft_v, 'ctx', axis=0, tiled=True)  76.2 us
    all_gather x1, waiting for transfers between devices, local(): lax.all_gather(soft_k, 'ctx', axis=0, tiled=True)  50.7 us
    all_to_all x1, starting transfers between devices, local(): lax.all_to_all(part_key, 'ctx', split_axis=0, concat_axis=0, tiled=True)  38.5 us
    all_gather x1, blocking collectives, local(): lax.all_gather(block_lists, 'ctx', axis=0, tiled=True)  37.6 us
    add x31, other arithmetic, chain_join(): later[0][:, None, None] * earlier[1] + later[1]  32.7 us
    gather x1, local copies, waits for them, and re-layouts, local(): new_keys = jnp.where(usable, shard_piece[0][safe_index], empty_slot)  30.5 us
  transfers between devices with their start and end apart: 6, of which 3 were waited for; matrix products, arithmetic and copies ran while one was open for 19% of the time, Pallas kernels for 0%

commit v1 on v0

--- a/solution.py
+++ b/solution.py
@@ -7,6 +7,11 @@
 NSEL = 16
 epsilon = 1e-05
 exact_precision = lax.Precision.HIGHEST
+
+
+def all_by_exchange(x, mesh_axis, d):
+    sent = jnp.stack([x] * lax.axis_size(mesh_axis))
+    return jnp.concatenate(lax.all_to_all(sent, mesh_axis, 0, 0), axis=d)
 
 
 def carried_in(part, axis, combine, identity, reverse):
@@ -114,7 +119,7 @@
     root_mean = jnp.sqrt(squares / total_width + epsilon)
     norm_scale = norm_gain[None]
     all_lists, all_counts = (
-        lax.all_gather(block_lists, "ctx", axis=0, tiled=True),
+        all_by_exchange(block_lists, "ctx", 0),
         lax.all_gather(block_counts, "ctx", axis=0, tiled=True),
     )
     entries = blocks_here * NSEL

time: 773 us -> 747 us (0.966); the launches traced: 771 us -> 736 us
  blocking collectives: 239 us -> 200 us
  starting transfers between devices: 45.2 us -> 59.1 us
  waiting for transfers between devices: 256 us -> 245 us
    all_gather x1 -> x0, blocking collectives: 37.6 us -> none  [local(): lax.all_gather(block_lists, 'ctx', axis=0, tiled=True)]
    all_gather x1, waiting for transfers between devices: 76.2 us -> 63.7 us  [local(): lax.all_gather(soft_v, 'ctx', axis=0, tiled=True)]
    all_to_all x0 -> x1, starting transfers between devices: none -> 11.4 us  [all_by_exchange(): return jnp.concatenate(lax.all_to_all(sent, mesh_axis, 0, 0), axis=d)]
  transfers between devices with their start and end apart: 6 -> 7, of which waited for: 3 -> 3; matrix products, arithmetic and copies ran while one was open for 19% -> 20% of each run, Pallas kernels for 0% -> 0%
where the time goes in v1:
time: 747 us; the launch traced here: 736 us
  waiting for transfers between devices  245 us (33%)
  blocking collectives  200 us (27%)
  local copies, waits for them, and re-layouts  115 us (15%)
  starting transfers between devices  59.1 us (8%)
  other arithmetic  53.4 us (7%)
  matrix products  47.1 us (6%)
  between operations  15.8 us (2%)
    unnamed x2, blocking collectives  187 us
    all_to_all x1, waiting for transfers between devices, local(): lax.all_to_all(part_key, 'ctx', split_axis=0, concat_axis=0, tiled=True)  129 us
    all_gather x1, waiting for transfers between devices, local(): lax.all_gather(soft_v, 'ctx', axis=0, tiled=True)  63.7 us
    all_gather x1, waiting for transfers between devices, local(): lax.all_gather(soft_k, 'ctx', axis=0, tiled=True)  50.6 us
    all_to_all x1, starting transfers between devices, local(): lax.all_to_all(part_key, 'ctx', split_axis=0, concat_axis=0, tiled=True)  40.9 us
    add x31, other arithmetic, chain_join(): later[0][:, None, None] * earlier[1] + later[1]  32.7 us
    gather x1, local copies, waits for them, and re-layouts, local(): new_values = jnp.where(usable, shard_piece[1][safe_index], empty_slot)  30.5 us
    gather x1, local copies, waits for them, and re-layouts, local(): new_keys = jnp.where(usable, shard_piece[0][safe_index], empty_slot)  30.5 us
  transfers between devices with their start and end apart: 7, of which 3 were waited for; matrix products, arithmetic and copies ran while one was open for 20% of the time, Pallas kernels for 0%

profile of v1, /device:TPU:32, one launch (start us, length us, event | category | flops | bytes accessed | tf_op | source)
XLA Modules:
  0.0 735.8 jit_solution(5333332545220023563)
XLA Ops:
  11.0 2.2 fusion.51
  13.2 1.3 stack.2
  14.5 11.4 %all-to-all-start = ((s32[32,1,16]{2,1,0:T(1,128)}), s32[32,1,16]{2,1,0:T(1,128)S(1)}, u32[]{:S(2)}, u32[]{:S(2)}) async-start(s32[32,1,16]{2,1,0:T(1,128)} %stack.2), calls=%async_computation | async-start | bytes 32768 | tf_op jit(solution)/shard_map/all_to_all | solution.py:14
  29.8 1.3 add_bitcast_fusion
  31.1 63.7 %all-gather.10.cloned.1.call-done = bf16[4096,4,128]{2,1,0:T(4,128)(2,1)} async-done(((bf16[128,4,128]{2,1,0:T(4,128)(2,1)}), bf16[4096,4,128]{2,1,0:T(4,128)(2,1)}) %all-gather.10.cloned.1.call-update) | async-done | bytes 4194320 | tf_op jit(solution)/shard_map/all_gather | solution.py:142
  94.8 30.5 %gather_fusion.1 = bf16[4096,4,128]{2,1,0:T(4,128)(2,1)} fusion(bf16[4096,4,128]{2,1,0:T(4,128)(2,1)} %all-gather.10.cloned.1.call-done, s32[4096]{0:T(1024)S(1)} %fusion.73), kind=kCustom, calls=%fused_computation.3 | custom fusion | bytes 8404992 | tf_op jit(solution)/shard_map/gather | solution.py:151
  125.4 50.6 %all-gather.8.cloned.1.call-done = bf16[4096,4,128]{2,1,0:T(4,128)(2,1)} async-done(((bf16[128,4,128]{2,1,0:T(4,128)(2,1)}), bf16[4096,4,128]{2,1,0:T(4,128)(2,1)}) %all-gather.8.cloned.1.call-update) | async-done | bytes 4194320 | tf_op jit(solution)/shard_map/all_gather | solution.py:141
  176.0 30.5 %gather_fusion = bf16[4096,4,128]{2,1,0:T(4,128)(2,1)} fusion(bf16[4096,4,128]{2,1,0:T(4,128)(2,1)} %all-gather.8.cloned.1.call-done, s32[4096]{0:T(1024)S(1)} %fusion.73), kind=kCustom, calls=%fused_computation.2 | custom fusion | bytes 8404992 | tf_op jit(solution)/shard_map/gather | solution.py:150
  206.5 6.7 copy_select_fusion
  213.2 3.2 gather_fusion.3
  216.3 4.4 gather_fusion.2
  220.7 3.4 broadcast_select_fusion
  224.3 3.9 fusion.102
  228.2 2.7 fusion.24
  231.9 1.7 copy-done.1
  233.7 7.5 %fusion.18 = bf16[32,128,4,128]{3,0,2,1:T(8,128)(2,1)S(1)} fusion(f32[16,128,4,128]{3,1,0,2:T(8,128)S(1)} %bitcast.219, s32[16]{0:T(128)S(1)} %bitcast.232, pred[16]{0:T(512)(128)(4,1)S(1)} %iota_compare_fusion.4), kind=kOutput, calls=%fused_computation.32 | convolution fusion | flops 404751360 | bytes 8388688 | tf_op jit(solution)/shard_map/oe,exhd->oxhd/dot_general | solution.py:181
  241.2 4.2 copy.264
  245.4 6.6 all-to-all-start.1
  253.6 170.3 %all-reduce.1 = f32[128]{0:T(128)S(1)} all-reduce(f32[128]{0:T(128)S(1)} %dynamic-update-slice.1), channel_id=2, replica_groups=mesh['ctx'=32,'head'=8] {'ctx'}, use_global_device_ids=true, to_apply=%add.1 | all-reduce | flops 128 | bytes 1024
  424.7 17.2 %all-reduce = s32[32]{0:T(128)S(1)} all-reduce(s32[32]{0:T(128)S(1)} %dynamic-update-slice), channel_id=1, replica_groups=mesh['ctx'=32,'head'=8] {'ctx'}, use_global_device_ids=true, to_apply=%add | all-reduce | flops 32 | bytes 256
  443.8 1.1 while.26
  443.8 1.1 bitcast_add_fusion.4
  445.5 4.6 fusion.12
  450.2 2.0 multiply_reduce_fusion.1
  452.2 12.9 %all-reduce.2 = (f32[128]{0:T(128)S(1)}, f32[128]{0:T(128)S(1)}) all-reduce(f32[128]{0:T(128)S(1)} %get-tuple-element.174, f32[128]{0:T(128)S(1)} %get-tuple-element.173), channel_id=1, replica_groups=mesh['ctx'=32,'head'=8] {'head'}, use_global_device_ids=true, to_apply=%region_10.12 | all-reduce | flops 256 | bytes 2048 | tf_op jit(solution)/shard_map/psum | solution.py:201
  465.1 1.2 multiply_subtract_fusion
  466.3 2.1 fusion.48
  469.3 1.8 copy.292
  471.2 1.9 fusion.43
  473.1 3.1 fusion.9
  477.2 1.8 copy-done.2
  479.0 7.2 fusion.21
  486.2 4.1 copy.301
  490.3 40.9 %all-to-all-start.2 = ((bf16[32,128,4,128]{3,2,1,0:T(4,128)(2,1)}), bf16[32,128,4,128]{3,2,1,0:T(4,128)(2,1)}, u32[]{:S(2)}, u32[]{:S(2)}) async-start(bf16[32,128,4,128]{3,2,1,0:T(4,128)(2,1)} %copy.301), calls=%async_computation.2 | async-start | bytes 8388608 | tf_op jit(solution)/shard_map/all_to_all | solution.py:185
  531.3 2.4 fusion.42
  534.6 128.8 %all-to-all-done.2 = bf16[32,128,4,128]{3,2,1,0:T(4,128)(2,1)} async-done(((bf16[32,128,4,128]{3,2,1,0:T(4,128)(2,1)}), bf16[32,128,4,128]{3,2,1,0:T(4,128)(2,1)}, u32[]{:S(2)}, u32[]{:S(2)}) %all-to-all-start.2) | async-done | bytes 4194336 | tf_op jit(solution)/shard_map/all_to_all | solution.py:185
  663.3 4.6 fusion.10
  673.6 53.2 %while.27 = (s32[]{:T(128)}, f32[4,128,128]{2,1,0:T(8,128)S(1)}, s32[]{:T(128)}, f32[32,4]{1,0:T(8,128)}, f32[32,4,128,128]{3,2,1,0:T(8,128)}, /*index=5*/s32[]{:T(128)}, s32[]{:T(128)}, s32[]{:T(128)}, s32[]{:T(128)}) while((s32[]{:T(128)}, f32[4,128,128]{2,1,0:T(8,128)S(1)}, s32[]{:T(128)}, f32[32,4]{1,0:T(8,128)}, ...), condition=%wide.region_12.14_spmd, body=%wide.region_11.13_spmd.sunk | while | flops 131078 | bytes 786635 | solution.py:30
  674.3 1.1 bitcast_add_fusion.5
  676.1 1.1 bitcast_add_fusion.5
  677.9 1.1 bitcast_add_fusion.5
  679.7 1.1 bitcast_add_fusion.5
  681.4 1.1 bitcast_add_fusion.5
  683.2 1.1 bitcast_add_fusion.5
  685.0 1.1 bitcast_add_fusion.5
  686.7 1.1 bitcast_add_fusion.5
  690.3 1.1 bitcast_add_fusion.5
  692.1 1.1 bitcast_add_fusion.5
  (167 shorter events, 65.0 us)
Async XLA Ops:
  7.2 217.2 %copy-start = (bf16[128,4,128]{2,1,0:T(4,128)(2,1)S(1)}, bf16[128,4,128]{2,1,0:T(4,128)(2,1)}, u32[]{:S(2)}) copy-start(bf16[128,4,128]{2,1,0:T(4,128)(2,1)} %param.22) | copy-start | bytes 393220
  7.2 87.6 %all-gather.10.cloned.1.call-start = ((), (), s32[]{:S(2)}) async-start(), calls=%async_computation.4 | async-start | bytes 4325376 | tf_op jit(solution)/shard_map/all_gather | solution.py:142
  7.9 168.1 %all-gather.8.cloned.1.call-start = ((), (), s32[]{:S(2)}) async-start(), calls=%async_computation.3 | async-start | bytes 4325376 | tf_op jit(solution)/shard_map/all_gather | solution.py:141
  8.7 435.1 %all-gather.12.cloned.1.call-start = ((), (), s32[]{:S(2)}) async-start(), calls=%async_computation.5 | async-start | bytes 8650752 | tf_op jit(solution)/shard_map/all_gather | solution.py:21
  9.7 432.2 %copy-start.15 = (f32[4,128]{1,0:T(4,128)}, f32[4,128]{1,0:T(4,128)S(1)}, u32[]{:S(2)}) copy-start(f32[4,128]{1,0:T(4,128)S(1)} %reduce_window_sum.11) | copy-start | bytes 6148
  10.5 0.6 copy-start.17
  14.5 230.9 %all-to-all-start = ((s32[32,1,16]{2,1,0:T(1,128)}), s32[32,1,16]{2,1,0:T(1,128)S(1)}, u32[]{:S(2)}, u32[]{:S(2)}) async-start(s32[32,1,16]{2,1,0:T(1,128)} %stack.2), calls=%async_computation | async-start | bytes 32768 | tf_op jit(solution)/shard_map/all_to_all | solution.py:14
  26.8 197.5 %copy-start.13 = (bf16[128,4,128]{2,0,1:T(8,128)(2,1)}, bf16[128,4,128]{2,0,1:T(8,128)(2,1)S(1)}, u32[]{:S(2)}) copy-start(bf16[128,4,128]{2,0,1:T(8,128)(2,1)S(1)} %copy.404) | copy-start | bytes 393220
  27.5 206.2 %copy-start.23 = (pred[16]{0:T(512)(128)(4,1)}, pred[16]{0:T(512)(128)(4,1)S(1)}, u32[]{:S(2)}) copy-start(pred[16]{0:T(512)(128)(4,1)S(1)} %iota_compare_fusion.4) | copy-start | bytes 52
  224.3 3.9 copy-start.3
  228.2 2.7 copy-start.25
  228.2 2.7 copy-start.7
  231.6 2.0 copy-start.1
  231.7 2.0 copy-start.21
  245.4 6.7 copy-start.27
  245.4 196.6 %copy-start.5 = (bf16[128,4,128]{2,1,0:T(4,128)(2,1)S(1)}, bf16[128,4,128]{2,1,0:T(4,128)(2,1)}, u32[]{:S(2)}) copy-start(bf16[128,4,128]{2,1,0:T(4,128)(2,1)} %param.17) | copy-start | bytes 393220
  245.4 196.6 %copy-start.6 = (bf16[128,4,128]{2,1,0:T(4,128)(2,1)S(1)}, bf16[128,4,128]{2,1,0:T(4,128)(2,1)}, u32[]{:S(2)}) copy-start(bf16[128,4,128]{2,1,0:T(4,128)(2,1)} %param.18) | copy-start | bytes 393220
  245.4 196.8 %copy-start.4 = (bf16[128,4,128]{2,1,0:T(4,128)(2,1)S(1)}, bf16[128,4,128]{2,1,0:T(4,128)(2,1)}, u32[]{:S(2)}) copy-start(bf16[128,4,128]{2,1,0:T(4,128)(2,1)} %param.19) | copy-start | bytes 393220
  245.4 200.1 %all-to-all-start.1 = ((bf16[32,128,4,128]{3,2,1,0:T(4,128)(2,1)}), bf16[32,128,4,128]{3,2,1,0:T(4,128)(2,1)}, u32[]{:S(2)}, u32[]{:S(2)}) async-start(bf16[32,128,4,128]{3,2,1,0:T(4,128)(2,1)} %copy.264), calls=%async_computation.1 | async-start | bytes 8388608 | tf_op jit(solution)/shard_map/all_to_all | solution.py:186
  252.0 421.6 %all-gather.14.cloned.1.call-start = ((), (), s32[]{:S(2)}) async-start(), calls=%async_computation.6 | async-start | bytes 8650752 | tf_op jit(solution)/shard_map/all_gather | solution.py:21
  442.2 2.7 copy-start.9
  444.9 0.6 copy-start.20
  445.5 4.7 copy-start.11
  471.2 1.9 copy-start.8
  471.2 1.9 copy-start.26
  476.9 2.1 copy-start.2
  476.9 2.1 copy-start.22
  476.9 2.1 copy-start.24
  490.3 41.0 %copy-start.14 = (bf16[128,4,128]{2,0,1:T(8,128)(2,1)S(1)}, bf16[128,4,128]{2,0,1:T(8,128)(2,1)}, u32[]{:S(2)}) copy-start(bf16[128,4,128]{2,0,1:T(8,128)(2,1)} %copy-done.13) | copy-start | bytes 393220
  490.3 173.0 %all-to-all-start.2 = ((bf16[32,128,4,128]{3,2,1,0:T(4,128)(2,1)}), bf16[32,128,4,128]{3,2,1,0:T(4,128)(2,1)}, u32[]{:S(2)}, u32[]{:S(2)}) async-start(bf16[32,128,4,128]{3,2,1,0:T(4,128)(2,1)} %copy.301), calls=%async_computation.2 | async-start | bytes 8388608 | tf_op jit(solution)/shard_map/all_to_all | solution.py:185
  533.7 136.0 %copy-start.12 = (bf16[128,4,128]{2,0,1:T(8,128)(2,1)S(1)}, bf16[128,4,128]{2,0,1:T(8,128)(2,1)}, u32[]{:S(2)}) copy-start(bf16[128,4,128]{2,0,1:T(8,128)(2,1)} %get-tuple-element.199) | copy-start | bytes 393220
  533.7 136.7 %copy-start.16 = (f32[4,128]{1,0:T(4,128)S(1)}, f32[4,128]{1,0:T(4,128)}, u32[]{:S(2)}) copy-start(f32[4,128]{1,0:T(4,128)} %copy-done.15) | copy-start | bytes 6148
  533.8 137.4 %copy-start.19 = (f32[128,4]{0,1:T(4,128)S(1)}, f32[128,4]{0,1:T(4,128)}, u32[]{:S(2)}) copy-start(f32[128,4]{0,1:T(4,128)} %get-tuple-element.202) | copy-start | bytes 6148
  534.6 138.4 %copy-start.10 = (f32[4,128,128]{2,1,0:T(8,128)S(1)}, f32[4,128,128]{2,1,0:T(8,128)}, u32[]{:S(2)}) copy-start(f32[4,128,128]{2,1,0:T(8,128)} %copy-done.9) | copy-start | bytes 786436
  670.5 56.4 %copy-start.18 = (f32[128,4]{0,1:T(4,128)S(1)}, f32[128,4]{0,1:T(4,128)}, u32[]{:S(2)}) copy-start(f32[128,4]{0,1:T(4,128)} %copy-done.17) | copy-start | bytes 6148
Sparse Core Ops, SparseCore 0:
  10.6 84.1 all-gather.9
  97.4 78.5 all-gather.7
  178.6 148.6 all-gather.11
  468.5 195.7 all-gather.13
